TPU v7x, 32 devices: a whole 2x2x4 slice. The times are simulated.
32 devices in a mesh: groups: 2 (over x), expert: 16 (over z, y, core).
Axes of the slice: x: 2, y: 2, z: 4, core: 2. Of those that a mesh axis runs over, the one named last changes fastest.
Arguments:
- routes: int32 [2, 2048, 8], P(None, ('groups', 'expert')), parts along dimension 1, may hold values from 0 to 31, as said below
- gate_weights: float32 [2, 2048, 8], P(None, ('groups', 'expert')), parts along dimension 1, may hold values from 0.05 to 0.5
- grad_out: bfloat16 [2, 2048, 2048], P(None, ('groups', 'expert')), parts along dimension 1, may hold values from -6 to 6
- saved_hidden: bfloat16 [4, 32, 384, 768], P('groups', 'expert'), parts along dimension 0, may hold values from -20 to 20
- down_weight: bfloat16 [32, 768, 2048], P('expert'), may hold values from -0.21875 to 0.21875
Outputs:
- hidden_grad: bfloat16 [2, 2048, 8, 768], P(None, ('groups', 'expert')), parts along dimension 1
- update: bfloat16 [32, 1536, 2048], P('expert', 'groups'), parts along dimension 1
There are 2 independent parts, one for each index of `groups`. A program takes and returns all parts, laid end to end along the dimension named above; an argument that names none is the same for every part. Nothing has to cross between parts.
Inputs may be any that keep to these rules, and one draw needn't show every extreme that they name: `routes`: each token names 8 different experts. In each micro-batch the 64 tokens of one source name any expert at most 24 times, and some expert exactly 24 times by the tokens of every source.
All inputs are finite; a program needn't handle non-finite values.
Results may differ from a plain program's by a relative error of at most 0.011.
Values may be sent and summed in bfloat16 or wider, within the bound.
No kernel may reach another device: no remote copies, remote signals or barrier semaphores. Data moves between devices by JAX's collectives and lax.ppermute only.
A program may use at most 128 MiB of HBM per device.

v0:
```python
import math
import jax
import jax.numpy as jnp
from jax import lax
from jax.sharding import PartitionSpec as P

COEF_A = 3.4445
COEF_B = -4.775
COEF_C = 2.0315


def pick_rows(source_table, row_index):
    return jnp.take(source_table, row_index, axis=0)


def row_places(routes, capacity, experts):
    matches = (routes[..., None] == jnp.arange(experts, dtype=jnp.int32)).astype(jnp.int32)
    per_token = jnp.sum(matches, axis=2)
    earlier = jnp.cumsum(per_token, axis=1) - per_token
    slot_index = jnp.sum(matches * earlier[:, :, None, :], axis=3)
    return routes * capacity + slot_index


def fill_slots(places, gate_weights, grad_out, slot_total):
    batches, tokens, top_count = places.shape
    flat_place = places.reshape(batches, 1, tokens * top_count)
    target = jnp.arange(slot_total, dtype=jnp.int32)[None, :, None]
    matched = flat_place == target
    token_ids = (jnp.arange(tokens * top_count, dtype=jnp.int32) // top_count)[None, None, :]
    source_token = jnp.sum(jnp.where(matched, token_ids, 0), axis=2)
    slot_gate = jnp.sum(
        jnp.where(matched, gate_weights.reshape(batches, 1, tokens * top_count), 0.0), axis=2
    )
    picked_rows = jax.vmap(pick_rows)(grad_out, source_token)
    return (slot_gate[:, :, None] * picked_rows.astype(jnp.float32)).astype(jnp.bfloat16)


def orthogonal_step(weight_grad, model_width):
    hidden_width = weight_grad.shape[1]
    gram_raw = jnp.einsum(
        "efd,egd->efg", weight_grad, weight_grad, preferred_element_type=jnp.float32
    )
    frob_norm = jnp.sqrt(jnp.sum(gram_raw * gram_raw, axis=(1, 2))) + 1e-06
    gram_unit = gram_raw / frob_norm[:, None, None]
    gram_half = gram_unit.astype(jnp.bfloat16)
    identity = jnp.eye(hidden_width, dtype=jnp.float32)[None]
    square_first = jnp.einsum(
        "efg,egh->efh", gram_half, gram_half, preferred_element_type=jnp.float32
    )
    poly_first = (COEF_A * identity + COEF_B * gram_unit + COEF_C * square_first).astype(
        jnp.bfloat16
    )
    left_product = jnp.einsum(
        "efg,egh->efh", poly_first, gram_half, preferred_element_type=jnp.float32
    ).astype(jnp.bfloat16)
    gram_next = jnp.einsum(
        "efg,egh->efh", left_product, poly_first, preferred_element_type=jnp.float32
    )
    next_half = gram_next.astype(jnp.bfloat16)
    square_next = jnp.einsum(
        "efg,egh->efh", next_half, next_half, preferred_element_type=jnp.float32
    )
    poly_next = (COEF_A * identity + COEF_B * gram_next + COEF_C * square_next).astype(jnp.bfloat16)
    product = jnp.einsum("efg,egh->efh", poly_next, poly_first, preferred_element_type=jnp.float32)
    scaling = math.sqrt(model_width) / jnp.sqrt(frob_norm)
    combined = (product * scaling[:, None, None]).astype(jnp.bfloat16)
    return jnp.einsum(
        "efg,egd->efd", combined, weight_grad, preferred_element_type=jnp.float32
    ).astype(jnp.bfloat16)


def local(routes, gate_weights, grad_out, saved_hidden, down_weight):
    devices = lax.axis_size("expert")
    local_experts = down_weight.shape[0]
    hidden_width = down_weight.shape[1]
    model_width = down_weight.shape[2]
    experts = devices * local_experts
    batches = saved_hidden.shape[0]
    slot_count = saved_hidden.shape[2]
    capacity = slot_count // devices
    tokens = routes.shape[1]
    top_count = routes.shape[2]
    places = row_places(routes, capacity, experts)
    outgoing = fill_slots(places, gate_weights, grad_out, experts * capacity)
    outgoing = outgoing.reshape(batches, devices, local_experts, capacity, model_width)
    arrived = lax.all_to_all(outgoing, "expert", split_axis=1, concat_axis=3, tiled=True)
    received = arrived.reshape(batches, local_experts, slot_count, model_width)
    slot_grad = jnp.einsum(
        "mjsd,jfd->mjsf", received, down_weight, preferred_element_type=jnp.float32
    ).astype(jnp.bfloat16)
    returned = lax.all_to_all(
        slot_grad.reshape(batches, 1, local_experts, slot_count, hidden_width),
        "expert",
        split_axis=3,
        concat_axis=1,
        tiled=True,
    )
    back_table = returned.reshape(batches, experts * capacity, hidden_width)
    hidden_grad = jax.vmap(pick_rows)(back_table, places.reshape(batches, tokens * top_count))
    hidden_grad = hidden_grad.reshape(batches, tokens, top_count, hidden_width)
    weight_grad = jnp.einsum(
        "mjsf,mjsd->jfd", saved_hidden, received, preferred_element_type=jnp.float32
    ).astype(jnp.bfloat16)
    update = orthogonal_step(weight_grad, model_width)
    return (hidden_grad, update)


def solution(mesh):
    in_specs = (
        P(None, ("groups", "expert"), None),
        P(None, ("groups", "expert"), None),
        P(None, ("groups", "expert"), None),
        P("groups", "expert", None, None),
        P("expert", None, None),
    )
    out_specs = (P(None, ("groups", "expert"), None, None), P("expert", "groups", None))
    return jax.shard_map(local, mesh=mesh, in_specs=in_specs, out_specs=out_specs, check_vma=False)
```

profile of v0, /device:TPU:15, one launch (start us, length us, event | category | flops | bytes accessed | tf_op | source)
XLA Modules:
  0.0 294.3 jit_solution(15632452333136307427)
XLA Ops:
  0.7 0.9 convert_reduce_fusion
  1.7 0.1 reduce_window_sum.11
  1.8 0.8 select_reduce_fusion.2
  2.6 0.7 compare_and_fusion.1
  3.4 0.1 reshape.126
  3.5 0.4 select_reduce_fusion
  4.0 0.1 reduce_sum.53
  4.2 0.8 copy.45
  5.0 0.1 broadcast_in_dim.56
  5.1 0.4 select_reduce_fusion.1
  5.5 0.1 mul.60
  5.7 33.1 %gather_fusion = bf16[1536,2048]{1,0:T(8,128)(2,1)} fusion(bf16[2,64,2048]{2,1,0:T(8,128)(2,1)S(1)} %copy-done.2, s32[1536]{0:T(1024)S(1)} %reshape.131), kind=kCustom, calls=%fused_computation | custom fusion | bytes 12595200 | tf_op jit(solution)/shard_map/vmap(jit(_take))/gather | solution.py:13
  38.8 7.2 %multiply_convert_fusion = bf16[2,16,2,24,2048]{4,3,0,2,1:T(8,128)(2,1)} fusion(bf16[2,16,2,24,2048]{4,3,2,1,0:T(8,128)(2,1)} %bitcast.42, f32[2,16,2,24]{3,0,2,1:T(2,128)S(1)} %copy.46, pred[2,16,2,24]{3,0,2,1:T(4,128)(4,1)S(1)} %copy.47), kind=kLoop, calls=%fused_computation.3 | loop fusion | flops 12582912 | bytes 12590592 | tf_op jit(solution)/shard_map/convert_element_type | solution.py:35
  45.9 6.5 %all-to-all-start = ((bf16[2,16,2,24,2048]{4,3,0,2,1:T(8,128)(2,1)}), bf16[2,16,2,24,2048]{4,3,0,2,1:T(8,128)(2,1)}, u32[]{:S(2)}, u32[]{:S(2)}) async-start(bf16[2,16,2,24,2048]{4,3,0,2,1:T(8,128)(2,1)} %multiply_convert_fusion), calls=%async_computation | async-start | bytes 12582912 | tf_op jit(solution)/shard_map/all_to_all | solution.py:86
  52.6 0.1 copy.43
  52.7 1.5 fusion.12
  54.3 135.6 %all-to-all-done = bf16[2,16,2,24,2048]{4,3,0,2,1:T(8,128)(2,1)} async-done(((bf16[2,16,2,24,2048]{4,3,0,2,1:T(8,128)(2,1)}), bf16[2,16,2,24,2048]{4,3,0,2,1:T(8,128)(2,1)}, u32[]{:S(2)}, u32[]{:S(2)}) %all-to-all-start) | async-done | bytes 6291488 | tf_op jit(solution)/shard_map/all_to_all | solution.py:86
  189.9 3.4 %copy.49 = bf16[2,1,2,16,24,2048]{5,4,3,0,2,1:T(8,128)(2,1)S(1)} copy(bf16[2,1,2,16,24,2048]{5,4,0,2,3,1:T(8,128)(2,1)} %bitcast.3) | data formatting | bytes 12582912 | tf_op jit(solution)/shard_map/all_to_all | solution.py:86
  193.2 8.1 %convert_bitcast_fusion = bf16[2,1,2,384,768]{4,3,0,2,1:T(8,128)(2,1)S(1)} fusion(bf16[2,2,384,2048]{3,2,0,1:T(8,128)(2,1)S(1)} %bitcast.44, bf16[2,768,2048]{2,1,0:T(8,128)(2,1)} %param.9), kind=kOutput, calls=%fused_computation.27 | convolution fusion | flops 4833017856 | bytes 14942208 | tf_op jit(solution)/shard_map/mjsd,jfd->mjsf/dot_general | solution.py:88
  201.4 7.3 %bitcast_convert_fusion = bf16[2,2048,768]{2,1,0:T(8,128)(2,1)} fusion(bf16[2,2,384,2048]{3,2,0,1:T(8,128)(2,1)S(1)} %bitcast.45, bf16[2,2,384,768]{3,2,1,0:T(8,128)(2,1)S(1)} %copy-done), kind=kOutput, calls=%fused_computation.2 | convolution fusion | flops 4834983936 | bytes 14942208 | tf_op jit(solution)/shard_map/mjsf,mjsd->jfd/dot_general | solution.py:101
  208.7 3.8 %copy.50 = bf16[2,1,2,384,768]{4,0,2,1,3:T(2,128)(2,1)} copy(bf16[2,1,2,384,768]{4,3,0,2,1:T(8,128)(2,1)S(1)} %convert_bitcast_fusion) | data formatting | bytes 4718592 | tf_op jit(solution)/shard_map/reshape | solution.py:92
  212.5 4.8 %all-to-all-start.1 = ((bf16[2,1,2,384,768]{4,0,2,1,3:T(2,128)(2,1)}), bf16[2,1,2,384,768]{4,0,2,1,3:T(2,128)(2,1)S(1)}, u32[]{:S(2)}, u32[]{:S(2)}) async-start(bf16[2,1,2,384,768]{4,0,2,1,3:T(2,128)(2,1)} %copy.50), calls=%async_computation.1 | async-start | bytes 4718592 | tf_op jit(solution)/shard_map/all_to_all | solution.py:91
  217.3 9.5 %multiply_reduce_fusion = (f32[2]{0:T(128)S(1)}, f32[2,768,768]{2,1,0:T(8,128)S(1)}) fusion(bf16[2,2048,768]{2,1,0:T(8,128)(2,1)} %bitcast_convert_fusion), kind=kOutput, calls=%fused_computation.10 | convolution fusion | flops 4834197504 | bytes 11010056 | tf_op jit(solution)/shard_map/efd,egd->efg/dot_general | solution.py:40
  226.8 2.2 copy-done.4
  228.9 3.8 %add_convert_fusion.1 = bf16[2,768,768]{2,1,0:T(8,128)(2,1)} fusion(f32[768,768]{1,0:T(8,128)S(1)} %copy-done.3, f32[2,768,768]{2,1,0:T(8,128)S(1)} %get-tuple-element.7, f32[2]{0:T(128)S(1)} %get-tuple-element.5), kind=kOutput, calls=%fused_computation.9 | convolution fusion | flops 1821376512 | bytes 9437192 | tf_op jit(solution)/shard_map/efg,egh->efh/dot_general | solution.py:47
  232.7 9.9 %fusion.7 = f32[2,768,768]{2,1,0:T(8,128)} fusion(bf16[2,768,768]{2,1,0:T(8,128)(2,1)} %add_convert_fusion.1, f32[2,768,768]{2,1,0:T(8,128)} %copy-done.4, f32[2]{0:T(128)S(1)} %get-tuple-element.5), kind=kOutput, calls=%fused_computation.20 | convolution fusion | flops 3627417600 | bytes 11796488 | tf_op jit(solution)/shard_map/efg,egh->efh/dot_general | solution.py:56
  242.6 13.0 %fusion.2 = f32[2,768,768]{2,1,0:T(8,128)} fusion(bf16[2,768,768]{2,1,0:T(8,128)(2,1)} %add_convert_fusion.1, f32[2,768,768]{2,1,0:T(8,128)} %fusion.7, f32[768,768]{1,0:T(8,128)} %fusion.12), kind=kOutput, calls=%fused_computation.15 | convolution fusion | flops 3630956544 | bytes 14155776 | tf_op jit(solution)/shard_map/efg,egh->efh/dot_general | solution.py:64
  255.6 10.3 %convolution_convert_fusion = bf16[2,768,2048]{2,1,0:T(8,128)(2,1)} fusion(bf16[2,2048,768]{2,1,0:T(8,128)(2,1)} %bitcast_convert_fusion, f32[2,768,768]{2,1,0:T(8,128)} %fusion.2, f32[2]{0:T(128)S(1)} %get-tuple-element.4), kind=kOutput, calls=%fused_computation.11 | convolution fusion | flops 4837343232 | bytes 17301512 | tf_op jit(solution)/shard_map/efg,egd->efd/dot_general | solution.py:67
  265.9 4.4 %all-to-all-done.1 = bf16[2,1,2,384,768]{4,0,2,1,3:T(2,128)(2,1)S(1)} async-done(((bf16[2,1,2,384,768]{4,0,2,1,3:T(2,128)(2,1)}), bf16[2,1,2,384,768]{4,0,2,1,3:T(2,128)(2,1)S(1)}, u32[]{:S(2)}, u32[]{:S(2)}) %all-to-all-start.1) | async-done | bytes 2359328 | tf_op jit(solution)/shard_map/all_to_all | solution.py:91
  270.3 1.7 copy.51
  272.0 19.4 %gather_fusion.1 = bf16[1024,768]{1,0:T(8,128)(2,1)} fusion(bf16[2,768,768]{2,1,0:T(8,128)(2,1)} %bitcast.40, s32[1024]{0:T(1024)S(1)} %bitcast.41), kind=kCustom, calls=%fused_computation.1 | custom fusion | bytes 3153920 | tf_op jit(solution)/shard_map/vmap(jit(_take))/gather | solution.py:13
  291.5 2.8 broadcast_select_fusion
  (23 shorter events, 0.5 us)
Async XLA Ops:
  0.6 200.7 %copy-start = (bf16[2,2,384,768]{3,2,1,0:T(8,128)(2,1)S(1)}, bf16[2,2,384,768]{3,2,1,0:T(8,128)(2,1)}, u32[]{:S(2)}) copy-start(bf16[2,2,384,768]{3,2,1,0:T(8,128)(2,1)} %param.8) | copy-start | bytes 7077892
  0.6 5.0 %copy-start.2 = (bf16[2,64,2048]{2,1,0:T(8,128)(2,1)S(1)}, bf16[2,64,2048]{2,1,0:T(8,128)(2,1)}, u32[]{:S(2)}) copy-start(bf16[2,64,2048]{2,1,0:T(8,128)(2,1)} %param.7) | copy-start | bytes 1572868
  45.9 143.9 %all-to-all-start = ((bf16[2,16,2,24,2048]{4,3,0,2,1:T(8,128)(2,1)}), bf16[2,16,2,24,2048]{4,3,0,2,1:T(8,128)(2,1)}, u32[]{:S(2)}, u32[]{:S(2)}) async-start(bf16[2,16,2,24,2048]{4,3,0,2,1:T(8,128)(2,1)} %multiply_convert_fusion), calls=%async_computation | async-start | bytes 12582912 | tf_op jit(solution)/shard_map/all_to_all | solution.py:86
  212.5 57.8 %all-to-all-start.1 = ((bf16[2,1,2,384,768]{4,0,2,1,3:T(2,128)(2,1)}), bf16[2,1,2,384,768]{4,0,2,1,3:T(2,128)(2,1)S(1)}, u32[]{:S(2)}, u32[]{:S(2)}) async-start(bf16[2,1,2,384,768]{4,0,2,1,3:T(2,128)(2,1)} %copy.50), calls=%async_computation.1 | async-start | bytes 4718592 | tf_op jit(solution)/shard_map/all_to_all | solution.py:91
  217.3 11.7 %copy-start.3 = (f32[768,768]{1,0:T(8,128)S(1)}, f32[768,768]{1,0:T(8,128)}, u32[]{:S(2)}) copy-start(f32[768,768]{1,0:T(8,128)} %fusion.12) | copy-start | bytes 7077892
  226.7 2.2 copy-start.4
  272.0 22.2 %copy-start.1 = (bf16[2,2,384,768]{3,2,1,0:T(8,128)(2,1)S(1)}, bf16[2,2,384,768]{3,2,1,0:T(8,128)(2,1)}, u32[]{:S(2)}) copy-start(bf16[2,2,384,768]{3,2,1,0:T(8,128)(2,1)} %param.8) | copy-start | bytes 7077892
where the time goes:
time: 295 us; the launch traced here: 294 us
  waiting for transfers between devices  140 us (47%)
  local copies, waits for them, and re-layouts  65.4 us (22%)
  matrix products  61.9 us (21%)
  other arithmetic  14.9 us (5%)
  starting transfers between devices  11.3 us (4%)
    all_to_all x1, waiting for transfers between devices, local(): lax.all_to_all(outgoing, 'expert', split_axis=1, concat_axis=3, tiled=True)  136 us
    gather x3, local copies, waits for them, and re-layouts, pick_rows(): return jnp.take(source_table, row_index, axis=0)  52.6 us
    dot_general x1, matrix products, orthogonal_step(): jnp.einsum('efg,egh->efh', poly_next, poly_first, preferred_element_type=...  13 us
    dot_general x1, matrix products, orthogonal_step(): jnp.einsum('efg,egd->efd', combined, weight_grad, preferred_element_type=...  10.3 us
    dot_general x1, matrix products, orthogonal_step(): jnp.einsum('efg,egh->efh', left_product, poly_first, preferred_element_ty...  9.89 us
    dot_general x1, matrix products, orthogonal_step(): jnp.einsum('efd,egd->efg', weight_grad, weight_grad, preferred_element_ty...  9.48 us
    dot_general x1, matrix products, local(): jnp.einsum('mjsd,jfd->mjsf', received, down_weight, preferred_element_typ...  8.13 us
    dot_general x1, matrix products, local(): jnp.einsum('mjsf,mjsd->jfd', saved_hidden, received, preferred_element_ty...  7.3 us
  transfers between devices with their start and end apart: 2, of which 2 were waited for; matrix products, arithmetic and copies ran while one was open for 16% of the time, Pallas kernels for 0%

commit v1 on v0

--- a/solution.py
+++ b/solution.py
@@ -83,7 +83,12 @@
     places = row_places(routes, capacity, experts)
     outgoing = fill_slots(places, gate_weights, grad_out, experts * capacity)
     outgoing = outgoing.reshape(batches, devices, local_experts, capacity, model_width)
-    arrived = lax.all_to_all(outgoing, "expert", split_axis=1, concat_axis=3, tiled=True)
+    arrived = jnp.concatenate(
+        lax.all_to_all(
+            jnp.stack(jnp.split(outgoing, lax.axis_size("expert"), axis=1)), "expert", 0, 0
+        ),
+        axis=3,
+    )
     received = arrived.reshape(batches, local_experts, slot_count, model_width)
     slot_grad = jnp.einsum(
         "mjsd,jfd->mjsf", received, down_weight, preferred_element_type=jnp.float32

time: 295 us -> 305 us (1.034)
  local copies, waits for them, and re-layouts: 65.4 us -> 77.7 us
    unnamed x12 -> x27, local copies, waits for them, and re-layouts: 2.99 us -> 14.6 us
    all_to_all x1 -> x0, local copies, waits for them, and re-layouts: 3.36 us -> none  [local(): lax.all_to_all(outgoing, 'expert', split_axis=1, concat_axis=3, tiled=True)]
    reshape x0 -> x1, local copies, waits for them, and re-layouts: none -> 3.36 us  [local(): jnp.concatenate(lax.all_to_all(jnp.stack(jnp.split(outgoing, lax.axis_siz...]
where the time goes in v1:
time: 305 us; the launch traced here: 304 us
  waiting for transfers between devices  140 us (46%)
  local copies, waits for them, and re-layouts  77.7 us (25%)
  matrix products  61.9 us (20%)
  other arithmetic  12.1 us (4%)
  starting transfers between devices  11.3 us (4%)
    all_to_all x1, waiting for transfers between devices, local(): lax.all_to_all(jnp.stack(jnp.split(outgoing, lax.axis_size('expert'), axi...  136 us
    gather x3, local copies, waits for them, and re-layouts, pick_rows(): return jnp.take(source_table, row_index, axis=0)  52.6 us
    unnamed x27, local copies, waits for them, and re-layouts  14.6 us
    dot_general x1, matrix products, orthogonal_step(): jnp.einsum('efg,egh->efh', poly_next, poly_first, preferred_element_type=...  13 us
    dot_general x1, matrix products, orthogonal_step(): jnp.einsum('efg,egd->efd', combined, weight_grad, preferred_element_type=...  10.3 us
    dot_general x1, matrix products, orthogonal_step(): jnp.einsum('efg,egh->efh', left_product, poly_first, preferred_element_ty...  9.89 us
    dot_general x1, matrix products, orthogonal_step(): jnp.einsum('efd,egd->efg', weight_grad, weight_grad, preferred_element_ty...  9.48 us
    dot_general x1, matrix products, local(): jnp.einsum('mjsd,jfd->mjsf', received, down_weight, preferred_element_typ...  8.13 us
  transfers between devices with their start and end apart: 2, of which 2 were waited for; matrix products, arithmetic and copies ran while one was open for 16% of the time, Pallas kernels for 0%

profile of v1, /device:TPU:15, one launch (start us, length us, event | category | flops | bytes accessed | tf_op | source)
XLA Modules:
  0.0 303.8 jit_solution(15014651220521665072)
XLA Ops:
  0.7 0.9 convert_reduce_fusion
  4.2 0.8 copy.75
  5.7 33.1 %gather_fusion = bf16[1536,2048]{1,0:T(8,128)(2,1)} fusion(bf16[2,64,2048]{2,1,0:T(8,128)(2,1)S(1)} %copy-done.2, s32[1536]{0:T(1024)S(1)} %reshape.130), kind=kCustom, calls=%fused_computation | custom fusion | bytes 12595200 | tf_op jit(solution)/shard_map/vmap(jit(_take))/gather | solution.py:13
  38.8 4.4 %multiply_convert_fusion = bf16[2,16,2,24,2048]{4,3,0,2,1:T(8,128)(2,1)S(1)} fusion(bf16[2,16,2,24,2048]{4,3,2,1,0:T(8,128)(2,1)} %bitcast.104, f32[2,16,2,24]{3,0,2,1:T(2,128)S(1)} %copy.76, pred[2,16,2,24]{3,0,2,1:T(4,128)(4,1)S(1)} %copy.77), kind=kLoop, calls=%fused_computation.3 | loop fusion | flops 12582912 | bytes 12590592 | tf_op jit(solution)/shard_map/convert_element_type | solution.py:35
  43.1 0.8 fusion.41
  43.9 0.8 fusion.40
  44.7 0.8 fusion.39
  45.5 0.8 fusion.38
  46.2 0.8 fusion.37
  47.0 0.8 fusion.36
  48.6 0.8 fusion.34
  49.3 0.8 fusion.33
  50.1 0.8 fusion.32
  50.9 0.8 fusion.31
  55.5 6.5 %all-to-all-start = ((bf16[16,2,1,2,24,2048]{5,4,1,3,2,0:T(8,128)(2,1)}), bf16[16,2,1,2,24,2048]{5,4,1,3,2,0:T(8,128)(2,1)}, u32[]{:S(2)}, u32[]{:S(2)}) async-start(bf16[16,2,1,2,24,2048]{5,4,1,3,2,0:T(8,128)(2,1)} %fusion.26), calls=%async_computation | async-start | bytes 12582912 | tf_op jit(solution)/shard_map/all_to_all | solution.py:87
  62.3 1.5 fusion.12
  63.8 135.6 %all-to-all-done = bf16[16,2,1,2,24,2048]{5,4,1,3,2,0:T(8,128)(2,1)} async-done(((bf16[16,2,1,2,24,2048]{5,4,1,3,2,0:T(8,128)(2,1)}), bf16[16,2,1,2,24,2048]{5,4,1,3,2,0:T(8,128)(2,1)}, u32[]{:S(2)}, u32[]{:S(2)}) %all-to-all-start) | async-done | bytes 6291488 | tf_op jit(solution)/shard_map/all_to_all | solution.py:87
  199.4 3.4 %copy.79 = bf16[2,1,2,16,24,2048]{5,4,3,0,2,1:T(8,128)(2,1)S(1)} copy(bf16[2,1,2,16,24,2048]{5,4,0,2,1,3:T(8,128)(2,1)} %bitcast.18) | data formatting | bytes 12582912 | tf_op jit(solution)/shard_map/reshape | solution.py:86
  202.8 8.1 %convert_bitcast_fusion = bf16[2,1,2,384,768]{4,3,0,2,1:T(8,128)(2,1)S(1)} fusion(bf16[2,2,384,2048]{3,2,0,1:T(8,128)(2,1)S(1)} %bitcast.106, bf16[2,768,2048]{2,1,0:T(8,128)(2,1)} %param.9), kind=kOutput, calls=%fused_computation.27 | convolution fusion | flops 4833017856 | bytes 14942208 | tf_op jit(solution)/shard_map/mjsd,jfd->mjsf/dot_general | solution.py:93
  211.0 7.3 %bitcast_convert_fusion = bf16[2,2048,768]{2,1,0:T(8,128)(2,1)} fusion(bf16[2,2,384,2048]{3,2,0,1:T(8,128)(2,1)S(1)} %bitcast.107, bf16[2,2,384,768]{3,2,1,0:T(8,128)(2,1)S(1)} %copy-done), kind=kOutput, calls=%fused_computation.2 | convolution fusion | flops 4834983936 | bytes 14942208 | tf_op jit(solution)/shard_map/mjsf,mjsd->jfd/dot_general | solution.py:106
  218.3 3.8 %copy.80 = bf16[2,1,2,384,768]{4,0,2,1,3:T(2,128)(2,1)} copy(bf16[2,1,2,384,768]{4,3,0,2,1:T(8,128)(2,1)S(1)} %convert_bitcast_fusion) | data formatting | bytes 4718592 | tf_op jit(solution)/shard_map/reshape | solution.py:97
  222.1 4.8 %all-to-all-start.1 = ((bf16[2,1,2,384,768]{4,0,2,1,3:T(2,128)(2,1)}), bf16[2,1,2,384,768]{4,0,2,1,3:T(2,128)(2,1)S(1)}, u32[]{:S(2)}, u32[]{:S(2)}) async-start(bf16[2,1,2,384,768]{4,0,2,1,3:T(2,128)(2,1)} %copy.80), calls=%async_computation.1 | async-start | bytes 4718592 | tf_op jit(solution)/shard_map/all_to_all | solution.py:96
  226.8 9.5 %multiply_reduce_fusion = (f32[2]{0:T(128)S(1)}, f32[2,768,768]{2,1,0:T(8,128)S(1)}) fusion(bf16[2,2048,768]{2,1,0:T(8,128)(2,1)} %bitcast_convert_fusion), kind=kOutput, calls=%fused_computation.10 | convolution fusion | flops 4834197504 | bytes 11010056 | tf_op jit(solution)/shard_map/efd,egd->efg/dot_general | solution.py:40
  236.4 2.2 copy-done.4
  238.5 3.8 %add_convert_fusion.1 = bf16[2,768,768]{2,1,0:T(8,128)(2,1)} fusion(f32[768,768]{1,0:T(8,128)S(1)} %copy-done.3, f32[2,768,768]{2,1,0:T(8,128)S(1)} %get-tuple-element.7, f32[2]{0:T(128)S(1)} %get-tuple-element.5), kind=kOutput, calls=%fused_computation.9 | convolution fusion | flops 1821376512 | bytes 9437192 | tf_op jit(solution)/shard_map/efg,egh->efh/dot_general | solution.py:47
  242.3 9.9 %fusion.7 = f32[2,768,768]{2,1,0:T(8,128)} fusion(bf16[2,768,768]{2,1,0:T(8,128)(2,1)} %add_convert_fusion.1, f32[2,768,768]{2,1,0:T(8,128)} %copy-done.4, f32[2]{0:T(128)S(1)} %get-tuple-element.5), kind=kOutput, calls=%fused_computation.20 | convolution fusion | flops 3627417600 | bytes 11796488 | tf_op jit(solution)/shard_map/efg,egh->efh/dot_general | solution.py:56
  252.2 13.0 %fusion.2 = f32[2,768,768]{2,1,0:T(8,128)} fusion(bf16[2,768,768]{2,1,0:T(8,128)(2,1)} %add_convert_fusion.1, f32[2,768,768]{2,1,0:T(8,128)} %fusion.7, f32[768,768]{1,0:T(8,128)} %fusion.12), kind=kOutput, calls=%fused_computation.15 | convolution fusion | flops 3630956544 | bytes 14155776 | tf_op jit(solution)/shard_map/efg,egh->efh/dot_general | solution.py:64
  265.2 10.3 %convolution_convert_fusion = bf16[2,768,2048]{2,1,0:T(8,128)(2,1)} fusion(bf16[2,2048,768]{2,1,0:T(8,128)(2,1)} %bitcast_convert_fusion, f32[2,768,768]{2,1,0:T(8,128)} %fusion.2, f32[2]{0:T(128)S(1)} %get-tuple-element.4), kind=kOutput, calls=%fused_computation.11 | convolution fusion | flops 4837343232 | bytes 17301512 | tf_op jit(solution)/shard_map/efg,egd->efd/dot_general | solution.py:67
  275.5 4.4 %all-to-all-done.1 = bf16[2,1,2,384,768]{4,0,2,1,3:T(2,128)(2,1)S(1)} async-done(((bf16[2,1,2,384,768]{4,0,2,1,3:T(2,128)(2,1)}), bf16[2,1,2,384,768]{4,0,2,1,3:T(2,128)(2,1)S(1)}, u32[]{:S(2)}, u32[]{:S(2)}) %all-to-all-start.1) | async-done | bytes 2359328 | tf_op jit(solution)/shard_map/all_to_all | solution.py:96
  279.9 1.7 copy.81
  281.6 19.4 %gather_fusion.1 = bf16[1024,768]{1,0:T(8,128)(2,1)} fusion(bf16[2,768,768]{2,1,0:T(8,128)(2,1)} %bitcast.102, s32[1024]{0:T(1024)S(1)} %bitcast.103), kind=kCustom, calls=%fused_computation.1 | custom fusion | bytes 3153920 | tf_op jit(solution)/shard_map/vmap(jit(_take))/gather | solution.py:13
  301.1 2.8 broadcast_select_fusion
  (39 shorter events, 8.1 us)
Async XLA Ops:
  0.6 210.3 %copy-start = (bf16[2,2,384,768]{3,2,1,0:T(8,128)(2,1)S(1)}, bf16[2,2,384,768]{3,2,1,0:T(8,128)(2,1)}, u32[]{:S(2)}) copy-start(bf16[2,2,384,768]{3,2,1,0:T(8,128)(2,1)} %param.8) | copy-start | bytes 7077892
  0.6 5.0 %copy-start.2 = (bf16[2,64,2048]{2,1,0:T(8,128)(2,1)S(1)}, bf16[2,64,2048]{2,1,0:T(8,128)(2,1)}, u32[]{:S(2)}) copy-start(bf16[2,64,2048]{2,1,0:T(8,128)(2,1)} %param.7) | copy-start | bytes 1572868
  55.5 143.9 %all-to-all-start = ((bf16[16,2,1,2,24,2048]{5,4,1,3,2,0:T(8,128)(2,1)}), bf16[16,2,1,2,24,2048]{5,4,1,3,2,0:T(8,128)(2,1)}, u32[]{:S(2)}, u32[]{:S(2)}) async-start(bf16[16,2,1,2,24,2048]{5,4,1,3,2,0:T(8,128)(2,1)} %fusion.26), calls=%async_computation | async-start | bytes 12582912 | tf_op jit(solution)/shard_map/all_to_all | solution.py:87
  222.1 57.8 %all-to-all-start.1 = ((bf16[2,1,2,384,768]{4,0,2,1,3:T(2,128)(2,1)}), bf16[2,1,2,384,768]{4,0,2,1,3:T(2,128)(2,1)S(1)}, u32[]{:S(2)}, u32[]{:S(2)}) async-start(bf16[2,1,2,384,768]{4,0,2,1,3:T(2,128)(2,1)} %copy.80), calls=%async_computation.1 | async-start | bytes 4718592 | tf_op jit(solution)/shard_map/all_to_all | solution.py:96
  226.8 11.7 %copy-start.3 = (f32[768,768]{1,0:T(8,128)S(1)}, f32[768,768]{1,0:T(8,128)}, u32[]{:S(2)}) copy-start(f32[768,768]{1,0:T(8,128)} %fusion.12) | copy-start | bytes 7077892
  236.3 2.2 copy-start.4
  281.6 22.2 %copy-start.1 = (bf16[2,2,384,768]{3,2,1,0:T(8,128)(2,1)S(1)}, bf16[2,2,384,768]{3,2,1,0:T(8,128)(2,1)}, u32[]{:S(2)}) copy-start(bf16[2,2,384,768]{3,2,1,0:T(8,128)(2,1)} %param.8) | copy-start | bytes 7077892
